TPU v7x, 512 devices: a whole 4x8x8 slice. The times are simulated.
512 devices in a mesh: dp: 32 (over z, x_hi, core), fsdp: 16 (over x_lo, y).
Axes of the slice: x: 4 (x_hi: 2, x_lo: 2; x = x_hi * 2 + x_lo), y: 8, z: 8, core: 2. Of those that a mesh axis runs over, the one named last changes fastest.
Arguments:
- tokens: bfloat16 [5120, 4608], P('fsdp'), may hold values from -12 to 12
- cotangent: bfloat16 [5120, 12288], P('fsdp', 'dp'), may hold values from -0.046875 to 0.046875
- gain: float32 [4608], replicated, may hold values from 0.5 to 1.5
- master: float32 [4608, 12288], P('fsdp', 'dp'), may hold values from -0.09375 to 0.09375
- momentum: float32 [4608, 12288], P('fsdp', 'dp'), may hold values from -3 to 3
Outputs:
- new_master: float32 [4608, 12288], P('fsdp', 'dp')
- new_momentum: float32 [4608, 12288], P('fsdp', 'dp')
All inputs are finite; a program needn't handle non-finite values.
Results may differ from a plain program's by a relative error of at most 0.0024.
Values may be sent and summed in bfloat16 or wider, within the bound.
A program may use at most 64 MiB of HBM per device.

v0:
```python
import math
import jax
import jax.numpy as jnp
from jax import lax
from jax.sharding import PartitionSpec as P

FF = 12288
inv_root_two = 1.0 / math.sqrt(2.0)
inv_root_two_pi = 1.0 / math.sqrt(2.0 * math.pi)


def norm_rows(tokens, gain):
    values = tokens.astype(jnp.float32)
    meansq = jnp.mean(values * values, axis=1, keepdims=True)
    return (values * lax.rsqrt(meansq + 1e-06) * gain).astype(jnp.bfloat16)


def slope_of(pre):
    cdf = 0.5 * (1.0 + jax.scipy.special.erf(pre * inv_root_two))
    return cdf + pre * jnp.exp(-0.5 * pre * pre) * inv_root_two_pi


def local(tokens, cotangent, gain, master, momentum):
    own_rows = master.shape[0]
    own_tokens = tokens.shape[0]
    n_shard = lax.axis_size("fsdp")
    n_copy = lax.axis_size("dp")
    share = own_tokens // n_copy
    along_rows = (((0,), (0,)), ((), ()))
    along_features = (((1,), (1,)), ((), ()))
    cot = cotangent.astype(jnp.float32)
    normed = norm_rows(tokens, gain)
    weights = lax.all_gather(master.astype(jnp.bfloat16), "fsdp", axis=0, tiled=True)
    mine = lax.dynamic_slice_in_dim(normed, lax.axis_index("dp") * share, share, 0)
    some = lax.all_gather(mine, "fsdp", axis=0, tiled=True)
    gram = lax.dot_general(some, normed, along_features, preferred_element_type=jnp.float32).astype(
        jnp.bfloat16
    )
    columns = lax.dynamic_slice_in_dim(some, lax.axis_index("fsdp") * own_rows, own_rows, 1)
    both = lax.all_gather(jnp.concatenate([gram, columns], axis=1), "dp", axis=0, tiled=True)
    both = both.reshape(n_copy, n_shard, share, own_tokens + own_rows)
    both = both.transpose(1, 0, 2, 3).reshape(n_shard * own_tokens, own_tokens + own_rows)
    gram_all = both[:, :own_tokens]
    columns_all = both[:, own_tokens:]

    def gathered(pre):
        dpre = (cot * slope_of(pre)).astype(jnp.bfloat16)
        return (dpre, lax.all_gather(dpre, "fsdp", axis=0, tiled=True))

    pre = jnp.dot(normed, weights, preferred_element_type=jnp.float32)
    dpre, dpre_all = gathered(pre)
    shift = lax.dot_general(gram_all, dpre_all, along_rows, preferred_element_type=jnp.float32)
    squares = lax.psum(jnp.sum(dpre.astype(jnp.float32) * shift), ("dp", "fsdp"))
    scale = math.sqrt(FF) / 4.0 / (jnp.sqrt(jnp.maximum(squares, 0.0)) + 1e-12)
    unused, dpre_two = gathered(pre + scale * shift)
    second = lax.dot_general(columns_all, dpre_two, along_rows, preferred_element_type=jnp.float32)
    new_momentum = 0.9 * momentum + second
    new_master = master - 0.002 * new_momentum
    return (new_master, new_momentum)


def solution(mesh):
    in_specs = (P("fsdp", None), P("fsdp", "dp"), P(), P("fsdp", "dp"), P("fsdp", "dp"))
    out_specs = (P("fsdp", "dp"), P("fsdp", "dp"))
    return jax.shard_map(local, mesh=mesh, in_specs=in_specs, out_specs=out_specs, check_vma=False)
```

profile of v0, /device:TPU:4, one launch (start us, length us, event | category | flops | bytes accessed | tf_op | source)
XLA Modules:
  0.0 539.6 jit_solution(4000123411859568000)
XLA Ops:
  7.2 0.0 all-gather.15.cloned.1.call-start
  7.2 0.0 copy-start
  7.2 2.6 fusion
  9.8 2.7 fusion.2
  12.5 0.7 dynamic-slice_bitcast_fusion
  13.2 0.0 all-gather.15.cloned.1.call-update
  13.2 0.0 all-gather.9.cloned.1.call-start
  13.3 0.7 convert_element_type.28
  14.0 0.0 all-gather.9.cloned.1.call-update
  14.0 0.0 all-gather.7.cloned.1.call-start
  14.1 77.9 %all-gather.15.cloned.1.call-done = bf16[16,10,4608]{2,1,0:T(8,128)(2,1)} async-done(((bf16[1,10,4608]{2,1,0:T(8,128)(2,1)}), bf16[16,10,4608]{2,1,0:T(8,128)(2,1)}) %all-gather.15.cloned.1.call-update) | async-done | bytes 1474576 | tf_op jit(solution)/shard_map/all_gather | solution.py:35
  92.0 2.8 reshape.22
  94.7 1.0 constant_dynamic-slice_fusion
  95.8 2.6 convolution_convert_fusion
  98.4 0.8 pad_maximum_fusion
  99.2 0.0 all-gather.7.cloned.1.call-update
  99.2 0.0 all-gather.11.cloned.1.call-start
  99.2 70.5 %all-gather.9.cloned.1.call-done = bf16[4608,384]{1,0:T(8,128)(2,1)} async-done(((bf16[288,384]{1,0:T(8,128)(2,1)}), bf16[4608,384]{1,0:T(8,128)(2,1)}) %all-gather.9.cloned.1.call-update) | async-done | bytes 3538960 | tf_op jit(solution)/shard_map/all_gather | solution.py:33
  169.7 4.5 fusion.10
  174.2 0.0 all-gather.11.cloned.1.call-update
  174.3 0.0 all-gather.13.cloned.1.call-start
  174.3 96.1 %all-gather.7.cloned.1.call-done = bf16[5120,608]{1,0:T(8,128)(2,1)} async-done(((bf16[160,608]{1,0:T(8,128)(2,1)}), bf16[5120,608]{1,0:T(8,128)(2,1)}) %all-gather.7.cloned.1.call-update) | async-done | bytes 6225936 | tf_op jit(solution)/shard_map/all_gather | solution.py:40
  270.4 12.8 %reshape.19 = bf16[32,16,10,608]{3,2,1,0:T(8,128)(2,1)} reshape(bf16[5120,608]{1,0:T(8,128)(2,1)} %all-gather.7.cloned.1.call-done) | data formatting | bytes 12451840 | tf_op jit(solution)/shard_map/reshape | solution.py:41
  283.2 9.3 %copy.8 = bf16[16,32,10,608]{3,2,1,0:T(8,128)(2,1)} copy(bf16[16,32,10,608]{3,2,0,1:T(8,128)(2,1)} %bitcast.9) | data formatting | bytes 12451840 | tf_op jit(solution)/shard_map/transpose | solution.py:42
  292.4 13.6 %reshape.20 = bf16[5120,608]{1,0:T(8,128)(2,1)} reshape(bf16[16,32,10,608]{3,2,1,0:T(8,128)(2,1)} %copy.8) | data formatting | bytes 12451840 | tf_op jit(solution)/shard_map/reshape | solution.py:42
  306.1 43.4 %all-gather.11.cloned.1.call-done = bf16[5120,384]{1,0:T(8,128)(2,1)} async-done(((bf16[320,384]{1,0:T(8,128)(2,1)}), bf16[5120,384]{1,0:T(8,128)(2,1)}) %all-gather.11.cloned.1.call-update) | async-done | bytes 3932176 | tf_op jit(solution)/shard_map/all_gather | solution.py:48
  349.5 5.8 %multiply_reduce_fusion = (f32[]{:T(128)}, f32[320,384]{1,0:T(8,128)S(1)}) fusion(bf16[320,384]{1,0:T(8,128)(2,1)S(1)} %copy-done.3, bf16[5120,384]{1,0:T(8,128)(2,1)} %all-gather.11.cloned.1.call-done, bf16[5120,608]{1,0:T(8,128)(2,1)} %reshape.20), kind=kOutput, calls=%fused_computation.25 | convolution fusion | flops 1258659840 | bytes 8601604 | tf_op jit(solution)/shard_map/dot_general | solution.py:52
  355.3 95.2 %psum.7 = f32[]{:T(128)} all-reduce(f32[]{:T(128)} %get-tuple-element.4), channel_id=1, replica_groups=mesh['dp'=32,'fsdp'=16] {'dp','fsdp'}, use_global_device_ids=true, to_apply=%region_2.0 | all-reduce | flops 1 | bytes 8 | tf_op jit(solution)/shard_map/psum | solution.py:53
  451.2 1.0 fusion.11
  452.2 0.0 all-gather.13.cloned.1.call-update
  452.2 73.9 %all-gather.13.cloned.1.call-done = bf16[5120,384]{1,0:T(8,128)(2,1)} async-done(((bf16[320,384]{1,0:T(8,128)(2,1)}), bf16[5120,384]{1,0:T(8,128)(2,1)}) %all-gather.13.cloned.1.call-update) | async-done | bytes 3932176 | tf_op jit(solution)/shard_map/all_gather | solution.py:48
  526.1 7.0 %multiply_subtract_fusion = (f32[288,384]{1,0:T(8,128)}, f32[288,384]{1,0:T(8,128)}) fusion(f32[288,384]{1,0:T(8,128)S(1)} %copy-done.1, bf16[5120,384]{1,0:T(8,128)(2,1)} %all-gather.13.cloned.1.call-done, bf16[5120,608]{1,0:T(8,128)(2,1)} %reshape.20, f32[288,384]{1,0:T(8,128)S(1)} %copy-done.4), kind=kOutput, calls=%fused_computation.26 | convolution fusion | flops 1132904448 | bytes 9633792 | tf_op jit(solution)/shard_map/dot_general | solution.py:56
  (10 shorter events, 0.0 us)
Async XLA Ops:
  7.2 84.8 %all-gather.15.cloned.1.call-start = ((), (), s32[]{:S(2)}) async-start(), calls=%async_computation.4 | async-start | bytes 2506752 | tf_op jit(solution)/shard_map/all_gather | solution.py:35
  7.2 6.1 %copy-start = (f32[288,384]{1,0:T(8,128)S(1)}, f32[288,384]{1,0:T(8,128)}, u32[]{:S(2)}) copy-start(f32[288,384]{1,0:T(8,128)} %param.8) | copy-start | bytes 1327108
  13.2 156.5 %all-gather.9.cloned.1.call-start = ((), (), s32[]{:S(2)}) async-start(), calls=%async_computation.1 | async-start | bytes 3760128 | tf_op jit(solution)/shard_map/all_gather | solution.py:33
  14.0 256.4 %all-gather.7.cloned.1.call-start = ((), (), s32[]{:S(2)}) async-start(), calls=%async_computation | async-start | bytes 6758400 | tf_op jit(solution)/shard_map/all_gather | solution.py:40
  99.2 250.3 %all-gather.11.cloned.1.call-start = ((), (), s32[]{:S(2)}) async-start(), calls=%async_computation.2 | async-start | bytes 4177920 | tf_op jit(solution)/shard_map/all_gather | solution.py:48
  174.3 351.8 %all-gather.13.cloned.1.call-start = ((), (), s32[]{:S(2)}) async-start(), calls=%async_computation.3 | async-start | bytes 4177920 | tf_op jit(solution)/shard_map/all_gather | solution.py:48
  292.4 57.0 %copy-start.3 = (bf16[320,384]{1,0:T(8,128)(2,1)S(1)}, bf16[320,384]{1,0:T(8,128)(2,1)}, u32[]{:S(2)}) copy-start(bf16[320,384]{1,0:T(8,128)(2,1)} %get-tuple-element.2) | copy-start | bytes 737284
  306.1 145.2 %copy-start.2 = (bf16[320,384]{1,0:T(8,128)(2,1)S(1)}, bf16[320,384]{1,0:T(8,128)(2,1)}, u32[]{:S(2)}) copy-start(bf16[320,384]{1,0:T(8,128)(2,1)} %param.6) | copy-start | bytes 737284
  306.1 220.0 %copy-start.1 = (f32[288,384]{1,0:T(8,128)S(1)}, f32[288,384]{1,0:T(8,128)}, u32[]{:S(2)}) copy-start(f32[288,384]{1,0:T(8,128)} %param.8) | copy-start | bytes 1327108
  306.1 220.0 %copy-start.4 = (f32[288,384]{1,0:T(8,128)S(1)}, f32[288,384]{1,0:T(8,128)}, u32[]{:S(2)}) copy-start(f32[288,384]{1,0:T(8,128)} %param.9) | copy-start | bytes 1327108
Sparse Core Ops, SparseCore 0:
  13.3 78.5 all-gather.14
  94.6 75.0 all-gather.8
  173.6 96.6 all-gather.6
  272.9 76.5 all-gather.10
  452.3 73.7 all-gather.12
where the time goes:
time: 541 us; the launch traced here: 540 us
  waiting for transfers between devices  362 us (67%)
  blocking collectives  95.2 us (18%)
  local copies, waits for them, and re-layouts  40.2 us (7%)
  matrix products  20 us (4%)
  between operations  14.6 us (3%)
  other arithmetic  7.69 us (1%)
    all_gather x2, waiting for transfers between devices, gathered(): return (dpre, lax.all_gather(dpre, 'fsdp', axis=0, tiled=True))  117 us
    all_gather x1, waiting for transfers between devices, local(): lax.all_gather(jnp.concatenate([gram, columns], axis=1), 'dp', axis=0, ti...  96.1 us
    psum x1, blocking collectives, local(): lax.psum(jnp.sum(dpre.astype(jnp.float32) * shift), ('dp', 'fsdp'))  95.2 us
    all_gather x1, waiting for transfers between devices, local(): some = lax.all_gather(mine, 'fsdp', axis=0, tiled=True)  77.9 us
    all_gather x1, waiting for transfers between devices, local(): lax.all_gather(master.astype(jnp.bfloat16), 'fsdp', axis=0, tiled=True)  70.5 us
    reshape x1, local copies, waits for them, and re-layouts, local(): both.transpose(1, 0, 2, 3)  13.6 us
    reshape x1, local copies, waits for them, and re-layouts, local(): both = both.reshape(n_copy, n_shard, share, own_tokens + own_rows)  12.8 us
  transfers between devices with their start and end apart: 5, of which 5 were waited for; matrix products, arithmetic and copies ran while one was open for 9% of the time, Pallas kernels for 0%

commit v1 on v0

--- a/solution.py
+++ b/solution.py
@@ -7,6 +7,19 @@
 FF = 12288
 inv_root_two = 1.0 / math.sqrt(2.0)
 inv_root_two_pi = 1.0 / math.sqrt(2.0 * math.pi)
+
+
+def corner_divide(s0, mesh_ax):
+    w_next = jnp.concatenate(
+        jax.lax.all_to_all(
+            jnp.stack([s0 for _ in range(jax.lax.axis_size(mesh_ax))], axis=0),
+            axis_name=mesh_ax,
+            concat_axis=0,
+            split_axis=0,
+        ),
+        axis=0,
+    )
+    return w_next
 
 
 def norm_rows(tokens, gain):
@@ -37,7 +50,7 @@
         jnp.bfloat16
     )
     columns = lax.dynamic_slice_in_dim(some, lax.axis_index("fsdp") * own_rows, own_rows, 1)
-    both = lax.all_gather(jnp.concatenate([gram, columns], axis=1), "dp", axis=0, tiled=True)
+    both = corner_divide(jnp.concatenate([gram, columns], axis=1), "dp")
     both = both.reshape(n_copy, n_shard, share, own_tokens + own_rows)
     both = both.transpose(1, 0, 2, 3).reshape(n_shard * own_tokens, own_tokens + own_rows)
     gram_all = both[:, :own_tokens]

time: 541 us -> 498 us (0.921)
  waiting for transfers between devices: 362 us -> 299 us
  blocking collectives: 95.2 us -> 106 us
  starting transfers between devices: 0.21 us -> 10.9 us
    all_gather x1 -> x0, waiting for transfers between devices: 96.1 us -> none  [local(): lax.all_gather(jnp.concatenate([gram, columns], axis=1), 'dp', axis=0, ti...]
    all_to_all x0 -> x1, waiting for transfers between devices: none -> 76 us  [corner_divide(): jax.lax.all_to_all(jnp.stack([s0 for _ in range(jax.lax.axis_size(mesh_ax...]
    all_gather x2, waiting for transfers between devices: 117 us -> 74.7 us  [gathered(): return (dpre, lax.all_gather(dpre, 'fsdp', axis=0, tiled=True))]
    reshape x1 -> x0, local copies, waits for them, and re-layouts: 12.8 us -> none  [local(): both = both.reshape(n_copy, n_shard, share, own_tokens + own_rows)]
    psum x1, blocking collectives: 95.2 us -> 106 us  [local(): lax.psum(jnp.sum(dpre.astype(jnp.float32) * shift), ('dp', 'fsdp'))]
    all_to_all x0 -> x1, starting transfers between devices: none -> 10.6 us  [corner_divide(): jax.lax.all_to_all(jnp.stack([s0 for _ in range(jax.lax.axis_size(mesh_ax...]
    all_to_all x0 -> x1, local copies, waits for them, and re-layouts: none -> 7.87 us  [corner_divide(): jax.lax.all_to_all(jnp.stack([s0 for _ in range(jax.lax.axis_size(mesh_ax...]
  transfers between devices with their start and end apart: 5 -> 5, of which waited for: 5 -> 4; matrix products, arithmetic and copies ran while one was open for 9% -> 9% of each run, Pallas kernels for 0% -> 0%
where the time goes in v1:
time: 498 us; the launch traced here: 497 us
  waiting for transfers between devices  299 us (60%)
  blocking collectives  106 us (21%)
  local copies, waits for them, and re-layouts  39.4 us (8%)
  matrix products  20.1 us (4%)
  between operations  14.6 us (3%)
  starting transfers between devices  10.9 us (2%)
  other arithmetic  7.01 us (1%)
    psum x1, blocking collectives, local(): lax.psum(jnp.sum(dpre.astype(jnp.float32) * shift), ('dp', 'fsdp'))  106 us
    all_gather x1, waiting for transfers between devices, local(): some = lax.all_gather(mine, 'fsdp', axis=0, tiled=True)  78 us
    all_to_all x1, waiting for transfers between devices, corner_divide(): jax.lax.all_to_all(jnp.stack([s0 for _ in range(jax.lax.axis_size(mesh_ax...  76 us
    all_gather x2, waiting for transfers between devices, gathered(): return (dpre, lax.all_gather(dpre, 'fsdp', axis=0, tiled=True))  74.7 us
    all_gather x1, waiting for transfers between devices, local(): lax.all_gather(master.astype(jnp.bfloat16), 'fsdp', axis=0, tiled=True)  70.2 us
    reshape x1, local copies, waits for them, and re-layouts, local(): both.transpose(1, 0, 2, 3)  13.6 us
    all_to_all x1, starting transfers between devices, corner_divide(): jax.lax.all_to_all(jnp.stack([s0 for _ in range(jax.lax.axis_size(mesh_ax...  10.6 us
    transpose x1, local copies, waits for them, and re-layouts, local(): both.transpose(1, 0, 2, 3)  10.2 us
  transfers between devices with their start and end apart: 5, of which 4 were waited for; matrix products, arithmetic and copies ran while one was open for 9% of the time, Pallas kernels for 0%

profile of v1, /device:TPU:4, one launch (start us, length us, event | category | flops | bytes accessed | tf_op | source)
XLA Modules:
  0.0 497.2 jit_solution(4451255214298321469)
XLA Ops:
  7.2 0.0 all-gather.12.cloned.1.call-start
  7.2 0.0 copy-start
  7.2 2.6 fusion
  9.8 2.7 fusion.2
  12.5 0.7 dynamic-slice_bitcast_fusion
  13.2 0.0 all-gather.12.cloned.1.call-update
  13.2 0.0 all-gather.6.cloned.1.call-start
  13.3 0.7 convert_element_type.28
  14.0 0.0 all-gather.6.cloned.1.call-update
  14.0 78.0 %all-gather.12.cloned.1.call-done = bf16[16,10,4608]{2,1,0:T(8,128)(2,1)} async-done(((bf16[1,10,4608]{2,1,0:T(8,128)(2,1)}), bf16[16,10,4608]{2,1,0:T(8,128)(2,1)}) %all-gather.12.cloned.1.call-update) | async-done | bytes 1474576 | tf_op jit(solution)/shard_map/all_gather | solution.py:48
  92.0 2.8 reshape.20
  94.7 1.0 constant_dynamic-slice_fusion
  95.7 2.6 convolution_convert_fusion
  98.4 0.1 pad_maximum_fusion
  98.5 3.2 stack.2
  101.7 10.6 %all-to-all-start = ((bf16[32,160,608]{2,1,0:T(8,128)(2,1)}), bf16[32,160,608]{2,1,0:T(8,128)(2,1)}, u32[]{:S(2)}, u32[]{:S(2)}) async-start(bf16[32,160,608]{2,1,0:T(8,128)(2,1)} %stack.2), calls=%async_computation | async-start | bytes 13107200 | tf_op jit(solution)/shard_map/all_to_all | solution.py:14
  112.3 0.0 all-gather.8.cloned.1.call-start
  112.3 70.2 %all-gather.6.cloned.1.call-done = bf16[4608,384]{1,0:T(8,128)(2,1)} async-done(((bf16[288,384]{1,0:T(8,128)(2,1)}), bf16[4608,384]{1,0:T(8,128)(2,1)}) %all-gather.6.cloned.1.call-update) | async-done | bytes 3538960 | tf_op jit(solution)/shard_map/all_gather | solution.py:46
  182.5 4.5 fusion.10
  187.1 0.0 all-gather.8.cloned.1.call-update
  187.1 0.2 all-gather.10.cloned.1.call-start
  187.3 76.0 %all-to-all-done = bf16[32,160,608]{2,1,0:T(8,128)(2,1)} async-done(((bf16[32,160,608]{2,1,0:T(8,128)(2,1)}), bf16[32,160,608]{2,1,0:T(8,128)(2,1)}, u32[]{:S(2)}, u32[]{:S(2)}) %all-to-all-start) | async-done | bytes 6225952 | tf_op jit(solution)/shard_map/all_to_all | solution.py:14
  263.3 7.9 %copy.8 = bf16[32,160,608]{2,0,1:T(8,128)(2,1)} copy(bf16[32,160,608]{2,1,0:T(8,128)(2,1)} %all-to-all-done) | data formatting | bytes 12451840 | tf_op jit(solution)/shard_map/all_to_all | solution.py:14
  271.2 10.2 %copy.9 = bf16[16,32,10,608]{3,2,1,0:T(8,128)(2,1)} copy(bf16[16,32,10,608]{3,1,2,0:T(8,128)(2,1)} %bitcast.11) | data formatting | bytes 12451840 | tf_op jit(solution)/shard_map/transpose | solution.py:55
  281.4 13.6 %reshape.18 = bf16[5120,608]{1,0:T(8,128)(2,1)} reshape(bf16[16,32,10,608]{3,2,1,0:T(8,128)(2,1)} %copy.9) | data formatting | bytes 12451840 | tf_op jit(solution)/shard_map/reshape | solution.py:55
  295.0 0.0 all-gather.8.cloned.1.call-done
  295.1 5.9 %multiply_reduce_fusion = (f32[]{:T(128)}, f32[320,384]{1,0:T(8,128)S(1)}) fusion(bf16[320,384]{1,0:T(8,128)(2,1)S(1)} %copy-done.3, bf16[5120,384]{1,0:T(8,128)(2,1)} %all-gather.8.cloned.1.call-done, bf16[5120,608]{1,0:T(8,128)(2,1)} %reshape.18), kind=kOutput, calls=%fused_computation.25 | convolution fusion | flops 1258659840 | bytes 8601604 | tf_op jit(solution)/shard_map/dot_general | solution.py:65
  301.0 106.3 %psum.7 = f32[]{:T(128)} all-reduce(f32[]{:T(128)} %get-tuple-element.4), channel_id=1, replica_groups=mesh['dp'=32,'fsdp'=16] {'dp','fsdp'}, use_global_device_ids=true, to_apply=%region_2.0 | all-reduce | flops 1 | bytes 8 | tf_op jit(solution)/shard_map/psum | solution.py:66
  408.0 1.0 fusion.11
  409.0 0.0 all-gather.10.cloned.1.call-update
  409.0 74.7 %all-gather.10.cloned.1.call-done = bf16[5120,384]{1,0:T(8,128)(2,1)} async-done(((bf16[320,384]{1,0:T(8,128)(2,1)}), bf16[5120,384]{1,0:T(8,128)(2,1)}) %all-gather.10.cloned.1.call-update) | async-done | bytes 3932176 | tf_op jit(solution)/shard_map/all_gather | solution.py:61
  483.7 7.0 %multiply_subtract_fusion = (f32[288,384]{1,0:T(8,128)}, f32[288,384]{1,0:T(8,128)}) fusion(f32[288,384]{1,0:T(8,128)S(1)} %copy-done.1, bf16[5120,384]{1,0:T(8,128)(2,1)} %all-gather.10.cloned.1.call-done, bf16[5120,608]{1,0:T(8,128)(2,1)} %reshape.18, f32[288,384]{1,0:T(8,128)S(1)} %copy-done.4), kind=kOutput, calls=%fused_computation.26 | convolution fusion | flops 1132904448 | bytes 9633792 | tf_op jit(solution)/shard_map/dot_general | solution.py:69
  (10 shorter events, 0.0 us)
Async XLA Ops:
  7.2 84.8 %all-gather.12.cloned.1.call-start = ((), (), s32[]{:S(2)}) async-start(), calls=%async_computation.4 | async-start | bytes 2506752 | tf_op jit(solution)/shard_map/all_gather | solution.py:48
  7.2 6.1 %copy-start = (f32[288,384]{1,0:T(8,128)S(1)}, f32[288,384]{1,0:T(8,128)}, u32[]{:S(2)}) copy-start(f32[288,384]{1,0:T(8,128)} %param.8) | copy-start | bytes 1327108
  13.2 169.3 %all-gather.6.cloned.1.call-start = ((), (), s32[]{:S(2)}) async-start(), calls=%async_computation.1 | async-start | bytes 3760128 | tf_op jit(solution)/shard_map/all_gather | solution.py:46
  101.7 161.6 %all-to-all-start = ((bf16[32,160,608]{2,1,0:T(8,128)(2,1)}), bf16[32,160,608]{2,1,0:T(8,128)(2,1)}, u32[]{:S(2)}, u32[]{:S(2)}) async-start(bf16[32,160,608]{2,1,0:T(8,128)(2,1)} %stack.2), calls=%async_computation | async-start | bytes 13107200 | tf_op jit(solution)/shard_map/all_to_all | solution.py:14
  112.3 182.8 %all-gather.8.cloned.1.call-start = ((), (), s32[]{:S(2)}) async-start(), calls=%async_computation.2 | async-start | bytes 4177920 | tf_op jit(solution)/shard_map/all_gather | solution.py:61
  187.1 296.6 %all-gather.10.cloned.1.call-start = ((), (), s32[]{:S(2)}) async-start(), calls=%async_computation.3 | async-start | bytes 4177920 | tf_op jit(solution)/shard_map/all_gather | solution.py:61
  281.4 13.6 %copy-start.3 = (bf16[320,384]{1,0:T(8,128)(2,1)S(1)}, bf16[320,384]{1,0:T(8,128)(2,1)}, u32[]{:S(2)}) copy-start(bf16[320,384]{1,0:T(8,128)(2,1)} %get-tuple-element.2) | copy-start | bytes 737284
  295.0 113.0 %copy-start.2 = (bf16[320,384]{1,0:T(8,128)(2,1)S(1)}, bf16[320,384]{1,0:T(8,128)(2,1)}, u32[]{:S(2)}) copy-start(bf16[320,384]{1,0:T(8,128)(2,1)} %param.6) | copy-start | bytes 737284
  295.0 188.6 %copy-start.1 = (f32[288,384]{1,0:T(8,128)S(1)}, f32[288,384]{1,0:T(8,128)}, u32[]{:S(2)}) copy-start(f32[288,384]{1,0:T(8,128)} %param.8) | copy-start | bytes 1327108
  295.0 188.6 %copy-start.4 = (f32[288,384]{1,0:T(8,128)S(1)}, f32[288,384]{1,0:T(8,128)}, u32[]{:S(2)}) copy-start(f32[288,384]{1,0:T(8,128)} %param.9) | copy-start | bytes 1327108
Sparse Core Ops, SparseCore 0:
  13.3 78.5 all-gather.11
  94.6 87.8 all-gather.5
  187.2 91.4 all-gather.7
  409.1 74.4 all-gather.9
